TPU v7x, 32 devices: a whole 2x2x4 slice. The times are simulated.
32 devices in a mesh: seq: 16 (over z, x, core), tp: 2 (over y).
Axes of the slice: x: 2, y: 2, z: 4, core: 2. Of those that a mesh axis runs over, the one named last changes fastest.
Arguments:
- normed_input: bfloat16 [2048, 4096], P(('seq', 'tp')), may hold values from -6 to 6
- output_gradient: bfloat16 [2048, 14336], P('seq', 'tp'), may hold values from -0.75 to 0.75
- adapter_down: bfloat16 [64, 16, 4096], P('seq', None, 'tp'), may hold values from -0.09375 to 0.09375
- adapter_up: bfloat16 [64, 16, 14336], P('seq', None, 'tp'), may hold values from -1.5 to 1.5
- adapter_of_block: int32 [16], P('seq'), may hold values from 0 to 63
- live_per_block: int32 [16], P('seq'), may hold values from 32 to 128, as said below
- adapter_home_row: int32 [64], replicated, may hold values from 0 to 63, each once
Outputs:
- adapter_output: bfloat16 [2048, 14336], P('seq', 'tp')
- input_gradient: bfloat16 [2048, 4096], P(('seq', 'tp'))
- down_gradient: float32 [64, 16, 4096], P('seq', None, 'tp')
- up_gradient: float32 [64, 16, 14336], P('seq', None, 'tp')
Inputs may be any that keep to these rules, and one draw needn't show every extreme that they name: `live_per_block`: every eighth block, counting from block 0, is full. `adapter_home_row`: each row appears once.
All inputs are finite; a program needn't handle non-finite values.
Results may differ from a plain program's by a relative error of at most 0.0051.
Values may be sent and summed in bfloat16 or wider, within the bound.
A program may use at most 128 MiB of HBM per device.

v0:
```python
import jax
import jax.numpy as jnp
from jax import lax
from jax.sharding import PartitionSpec as P

adapter_scale = 2.0


def per_device(
    normed_input,
    output_gradient,
    adapter_down,
    adapter_up,
    adapter_of_block,
    live_per_block,
    adapter_home_row,
):
    seq_count = lax.axis_size("seq")
    total_blocks = adapter_of_block.shape[0]
    token_rows = output_gradient.shape[0]
    block_length = token_rows // total_blocks
    adapters = adapter_home_row.shape[0]
    rank_projected = adapter_down.shape[1]
    width_slice = adapter_down.shape[2]
    hidden_slice = adapter_up.shape[2]
    all_a, all_b = (
        lax.all_gather(adapter_down, "seq", axis=0, tiled=True),
        lax.all_gather(adapter_up, "seq", axis=0, tiled=True),
    )
    chosen = (adapter_of_block[:, None] == jnp.arange(adapters, dtype=jnp.int32)[None, :]).astype(
        jnp.float32
    )
    chosen_low = chosen.astype(jnp.bfloat16)
    pick_a = jnp.einsum(
        "ba,ard->brd", chosen_low, all_a, preferred_element_type=jnp.float32
    ).astype(jnp.bfloat16)
    pick_b = jnp.einsum(
        "ba,arf->brf", chosen_low, all_b, preferred_element_type=jnp.float32
    ).astype(jnp.bfloat16)
    token_live_mask = (
        jnp.arange(block_length, dtype=jnp.int32)[None, :] < live_per_block[:, None]
    ).astype(jnp.float32)[:, :, None]
    g_blocks = output_gradient.reshape(total_blocks, block_length, hidden_slice)
    back_part = jnp.einsum("btf,brf->btr", g_blocks, pick_b, preferred_element_type=jnp.float32)
    back_part = back_part.reshape(total_blocks, block_length * rank_projected)
    x_tensor = lax.all_to_all(normed_input, "tp", split_axis=1, concat_axis=0, tiled=True)
    x_blocks = x_tensor.reshape(total_blocks, block_length, width_slice)
    down_part = jnp.einsum("btd,brd->btr", x_blocks, pick_a, preferred_element_type=jnp.float32)
    down_part = down_part.reshape(total_blocks, block_length * rank_projected)
    down_sum, backward_total = lax.psum((down_part, back_part), "tp")
    down_reduced = (
        down_sum.reshape(total_blocks, block_length, rank_projected) * token_live_mask
    ).astype(jnp.bfloat16)
    backward_reduced = (
        adapter_scale
        * backward_total.reshape(total_blocks, block_length, rank_projected)
        * token_live_mask
    ).astype(jnp.bfloat16)
    grad_tensor = jnp.einsum(
        "btr,brd->btd", backward_reduced, pick_a, preferred_element_type=jnp.float32
    )
    grad_tensor = grad_tensor.astype(jnp.bfloat16).reshape(token_rows, width_slice)
    input_gradient = lax.all_to_all(grad_tensor, "tp", split_axis=0, concat_axis=1, tiled=True)
    grad_a_blocks = jnp.einsum(
        "btr,btd->brd", backward_reduced, x_blocks, preferred_element_type=jnp.float32
    )
    adapter_output = adapter_scale * jnp.einsum(
        "btr,brf->btf", down_reduced, pick_b, preferred_element_type=jnp.float32
    )
    adapter_output = adapter_output.astype(jnp.bfloat16).reshape(token_rows, hidden_slice)
    up_gradient_blocks = adapter_scale * jnp.einsum(
        "btr,btf->brf", down_reduced, g_blocks, preferred_element_type=jnp.float32
    )
    block_row = jnp.dot(
        chosen, adapter_home_row.astype(jnp.float32), precision=lax.Precision.HIGHEST
    )
    slots_each = adapters // seq_count
    my_rows = (lax.axis_index("seq") * slots_each + jnp.arange(slots_each, dtype=jnp.int32)).astype(
        jnp.float32
    )
    piece_a = lax.all_gather(grad_a_blocks, "seq", axis=0, tiled=True)
    piece_b = lax.all_gather(up_gradient_blocks, "seq", axis=0, tiled=True)
    piece_rows = lax.all_gather(block_row, "seq", axis=0, tiled=True)
    match = (piece_rows[:, None] == my_rows[None, :]).astype(jnp.float32)
    following_down = jnp.einsum("ns,nrd->srd", match, piece_a, precision=lax.Precision.HIGHEST)
    following_up = jnp.einsum("ns,nrf->srf", match, piece_b, precision=lax.Precision.HIGHEST)
    return (adapter_output, input_gradient, following_down, following_up)


def solution(mesh):
    placed = (
        P(("seq", "tp"), None),
        P("seq", "tp"),
        P("seq", None, "tp"),
        P("seq", None, "tp"),
        P("seq"),
        P("seq"),
        P(),
    )
    return jax.shard_map(
        per_device,
        mesh=mesh,
        in_specs=placed,
        out_specs=(
            P("seq", "tp"),
            P(("seq", "tp"), None),
            P("seq", None, "tp"),
            P("seq", None, "tp"),
        ),
        check_vma=False,
    )
```

profile of v0, /device:TPU:0, one launch (start us, length us, event | category | flops | bytes accessed | tf_op | source)
XLA Modules:
  0.0 334.9 jit_solution(5447570768813441117)
XLA Ops:
  7.2 0.0 copy-start
  7.2 0.0 all-gather.7.cloned.1.call-start
  7.2 0.7 all-gather.7.cloned.1.call-update
  7.9 0.0 all-gather.9.cloned.1.call-start
  8.0 0.7 all-gather.9.cloned.1.call-update
  8.7 1.9 copy.62
  10.5 4.3 %all-to-all-start = ((bf16[64,2,2048]{2,0,1:T(8,128)(2,1)}), bf16[64,2,2048]{2,0,1:T(8,128)(2,1)S(1)}, u32[]{:S(2)}, u32[]{:S(2)}) async-start(bf16[64,2,2048]{2,0,1:T(8,128)(2,1)} %bitcast.50), calls=%async_computation | async-start | bytes 1048576 | tf_op jit(solution)/shard_map/all_to_all | solution.py:46
  14.8 0.0 all-gather.11.cloned.1.call-start
  16.1 0.1 mul.64
  16.2 0.1 mul.65
  16.3 0.1 mul.57
  16.4 0.1 mul.58
  16.5 46.8 %all-gather.7.cloned.1.call-done = bf16[64,16,2048]{2,1,0:T(8,128)(2,1)} async-done(((bf16[4,16,2048]{2,1,0:T(8,128)(2,1)}), bf16[64,16,2048]{2,1,0:T(8,128)(2,1)}) %all-gather.7.cloned.1.call-update) | async-done | bytes 4194320 | tf_op jit(solution)/shard_map/all_gather | solution.py:27
  63.3 6.7 %fusion.5 = bf16[1,16,2048]{2,0,1:T(2,128)(2,1)S(1)} fusion(bf16[64,16,2048]{2,1,0:T(8,128)(2,1)} %all-gather.7.cloned.1.call-done, s32[]{:T(128)} %bitcast.51), kind=kOutput, calls=%fused_computation.7 | convolution fusion | flops 4194496 | bytes 4259844 | tf_op jit(solution)/shard_map/ba,ard->brd/dot_general | solution.py:34
  70.0 0.0 all-to-all-done
  70.0 0.2 convolution_bitcast_fusion.1
  70.2 0.1 copy.32
  70.3 0.1 reshape.142
  70.4 107.1 %all-gather.9.cloned.1.call-done = bf16[64,16,7168]{2,1,0:T(8,128)(2,1)} async-done(((bf16[4,16,7168]{2,1,0:T(8,128)(2,1)}), bf16[64,16,7168]{2,1,0:T(8,128)(2,1)}) %all-gather.9.cloned.1.call-update) | async-done | bytes 14680080 | tf_op jit(solution)/shard_map/all_gather | solution.py:28
  177.5 20.9 %fusion = bf16[1,16,7168]{2,0,1:T(2,128)(2,1)S(1)} fusion(bf16[64,16,7168]{2,1,0:T(8,128)(2,1)} %all-gather.9.cloned.1.call-done, s32[]{:T(128)} %bitcast.52), kind=kOutput, calls=%fused_computation | convolution fusion | flops 14680256 | bytes 14909444 | tf_op jit(solution)/shard_map/ba,arf->brf/dot_general | solution.py:37
  198.4 0.0 copy-done
  198.4 0.0 copy-start.2
  198.4 0.0 copy-start.1
  198.4 0.6 convolution_bitcast_fusion
  199.0 0.1 copy.33
  199.1 0.1 reshape.143
  199.2 8.1 %all-reduce.1 = (f32[1,2048]{1,0:T(1,128)S(1)}, f32[1,2048]{1,0:T(1,128)S(1)}) all-reduce(f32[1,2048]{1,0:T(1,128)S(1)} %reshape.142, f32[1,2048]{1,0:T(1,128)S(1)} %reshape.143), channel_id=1, replica_groups=mesh['seq'=16,'tp'=2] {'tp'}, use_global_device_ids=true, to_apply=%region_0.0 | all-reduce | flops 4096 | bytes 32768 | tf_op jit(solution)/shard_map/psum | solution.py:50
  207.3 0.1 convert_reduce_fusion
  207.3 0.1 convert_element_type.81
  207.4 0.9 fusion.24
  208.3 0.0 all-gather.11.cloned.1.call-update
  208.3 0.0 all-gather.13.cloned.1.call-start
  208.4 0.1 convert_element_type.77
  208.4 1.2 convolution_multiply_fusion.1
  209.6 0.0 all-gather.13.cloned.1.call-update
  209.6 0.0 copy-done.2
  209.7 0.6 dynamic-slice
  210.2 0.0 copy-done.1
  210.2 0.6 fusion.19
  210.8 1.4 dynamic-update-slice
  212.2 30.0 %all-reduce = f32[16]{0:T(128)S(1)} all-reduce(f32[16]{0:T(128)S(1)} %dynamic-update-slice), channel_id=1, replica_groups=mesh['seq'=16,'tp'=2] {'seq'}, use_global_device_ids=true, to_apply=%add | all-reduce | flops 16 | bytes 128
  242.2 1.1 convolution_convert_fusion
  243.3 3.7 %all-to-all-start.1 = ((bf16[2,64,2048]{2,1,0:T(8,128)(2,1)}), bf16[2,64,2048]{2,1,0:T(8,128)(2,1)S(1)}, u32[]{:S(2)}, u32[]{:S(2)}) async-start(bf16[2,64,2048]{2,1,0:T(8,128)(2,1)} %bitcast.10), calls=%async_computation.1 | async-start | bytes 1048576 | tf_op jit(solution)/shard_map/all_to_all | solution.py:63
  247.0 1.8 fusion.2
  248.9 6.0 %all-to-all-done.1 = bf16[2,64,2048]{2,1,0:T(8,128)(2,1)S(1)} async-done(((bf16[2,64,2048]{2,1,0:T(8,128)(2,1)}), bf16[2,64,2048]{2,1,0:T(8,128)(2,1)S(1)}, u32[]{:S(2)}, u32[]{:S(2)}) %all-to-all-start.1) | async-done | bytes 524320 | tf_op jit(solution)/shard_map/all_to_all | solution.py:63
  254.9 0.8 copy.46
  255.7 0.0 all-gather.11.cloned.1.call-done
  255.7 3.6 %fusion.7 = f32[4,16,2048]{2,0,1:T(4,128)S(1)} fusion(f32[16,16,2048]{2,1,0:T(8,128)} %bitcast.59, f32[16]{0:T(128)S(1)} %all-reduce, f32[4]{0:T(128)S(1)} %add_convert_fusion), kind=kOutput, calls=%fused_computation.10 | convolution fusion | flops 25165888 | bytes 2621520 | tf_op jit(solution)/shard_map/ns,nrd->srd/dot_general | solution.py:85
  259.3 1.1 copy.37
  260.4 56.1 %all-gather.13.cloned.1.call-done = f32[256,7168]{1,0:T(8,128)} async-done(((f32[16,7168]{1,0:T(8,128)}), f32[256,7168]{1,0:T(8,128)}) %all-gather.13.cloned.1.call-update) | async-done | bytes 7340048 | tf_op jit(solution)/shard_map/all_gather | solution.py:82
  316.5 9.5 %fusion.3 = f32[4,16,7168]{2,0,1:T(4,128)S(1)} fusion(f32[16,16,7168]{2,1,0:T(8,128)} %bitcast.56, f32[16]{0:T(128)S(1)} %all-reduce, f32[4]{0:T(128)S(1)} %add_convert_fusion), kind=kOutput, calls=%fused_computation.5 | convolution fusion | flops 88080448 | bytes 9175120 | tf_op jit(solution)/shard_map/ns,nrf->srf/dot_general | solution.py:86
  326.1 2.3 copy.38
  (4 shorter events, 0.0 us)
Async XLA Ops:
  7.2 191.2 %copy-start = (bf16[128,7168]{1,0:T(8,128)(2,1)S(1)}, bf16[128,7168]{1,0:T(8,128)(2,1)}, u32[]{:S(2)}) copy-start(bf16[128,7168]{1,0:T(8,128)(2,1)} %param.8) | copy-start | bytes 5505028
  7.2 56.1 %all-gather.7.cloned.1.call-start = ((), (), s32[]{:S(2)}) async-start(), calls=%async_computation.2 | async-start | bytes 4456448 | tf_op jit(solution)/shard_map/all_gather | solution.py:27
  7.9 169.6 %all-gather.9.cloned.1.call-start = ((), (), s32[]{:S(2)}) async-start(), calls=%async_computation.3 | async-start | bytes 15597568 | tf_op jit(solution)/shard_map/all_gather | solution.py:28
  10.5 59.4 %all-to-all-start = ((bf16[64,2,2048]{2,0,1:T(8,128)(2,1)}), bf16[64,2,2048]{2,0,1:T(8,128)(2,1)S(1)}, u32[]{:S(2)}, u32[]{:S(2)}) async-start(bf16[64,2,2048]{2,0,1:T(8,128)(2,1)} %bitcast.50), calls=%async_computation | async-start | bytes 1048576 | tf_op jit(solution)/shard_map/all_to_all | solution.py:46
  14.8 240.9 %all-gather.11.cloned.1.call-start = ((), (), s32[]{:S(2)}) async-start(), calls=%async_computation.4 | async-start | bytes 2228224 | tf_op jit(solution)/shard_map/all_gather | solution.py:81
  198.4 11.3 %copy-start.2 = (u32[32]{0:T(128)S(1)}, u32[32]{0:T(128)}, u32[]{:S(2)}) copy-start(u32[32]{0:T(128)} %constant.20) | copy-start | bytes 388
  198.4 11.9 %copy-start.1 = (s32[64]{0:T(128)S(1)}, s32[64]{0:T(128)}, u32[]{:S(2)}) copy-start(s32[64]{0:T(128)} %param.13) | copy-start | bytes 772
  208.3 108.2 %all-gather.13.cloned.1.call-start = ((), (), s32[]{:S(2)}) async-start(), calls=%async_computation.5 | async-start | bytes 7798784 | tf_op jit(solution)/shard_map/all_gather | solution.py:82
  243.3 11.6 %all-to-all-start.1 = ((bf16[2,64,2048]{2,1,0:T(8,128)(2,1)}), bf16[2,64,2048]{2,1,0:T(8,128)(2,1)S(1)}, u32[]{:S(2)}, u32[]{:S(2)}) async-start(bf16[2,64,2048]{2,1,0:T(8,128)(2,1)} %bitcast.10), calls=%async_computation.1 | async-start | bytes 1048576 | tf_op jit(solution)/shard_map/all_to_all | solution.py:63
Sparse Core Ops, SparseCore 0:
  10.1 53.0 all-gather.6
  65.6 111.8 all-gather.8
  208.4 38.7 all-gather.10
  249.9 66.5 all-gather.12
where the time goes:
time: 335 us
  waiting for transfers between devices  217 us (65%)
  matrix products  46.5 us (14%)
  blocking collectives  38 us (11%)
  between operations  15.2 us (5%)
  local copies, waits for them, and re-layouts  9.04 us (3%)
  starting transfers between devices  8.09 us (2%)
    all_gather x1, waiting for transfers between devices, per_device(): lax.all_gather(adapter_up, 'seq', axis=0, tiled=True)  107 us
    all_gather x1, waiting for transfers between devices, per_device(): piece_b = lax.all_gather(up_gradient_blocks, 'seq', axis=0, tiled=True)  56.1 us
    all_gather x1, waiting for transfers between devices, per_device(): lax.all_gather(adapter_down, 'seq', axis=0, tiled=True)  46.8 us
    unnamed x1, blocking collectives  30 us
    dot_general x1, matrix products, per_device(): jnp.einsum('ba,arf->brf', chosen_low, all_b, preferred_element_type=jnp.f...  20.9 us
    dot_general x1, matrix products, per_device(): jnp.einsum('ns,nrf->srf', match, piece_b, precision=lax.Precision.HIGHEST)  9.53 us
    psum x1, blocking collectives, per_device(): down_sum, backward_total = lax.psum((down_part, back_part), 'tp')  8.06 us
    dot_general x1, matrix products, per_device(): jnp.einsum('ba,ard->brd', chosen_low, all_a, preferred_element_type=jnp.f...  6.7 us
  transfers between devices with their start and end apart: 6, of which 4 were waited for; matrix products, arithmetic and copies ran while one was open for 6% of the time, Pallas kernels for 0%

commit v1 on v0

--- a/solution.py
+++ b/solution.py
@@ -79,11 +79,27 @@
         jnp.float32
     )
     piece_a = lax.all_gather(grad_a_blocks, "seq", axis=0, tiled=True)
-    piece_b = lax.all_gather(up_gradient_blocks, "seq", axis=0, tiled=True)
     piece_rows = lax.all_gather(block_row, "seq", axis=0, tiled=True)
     match = (piece_rows[:, None] == my_rows[None, :]).astype(jnp.float32)
     following_down = jnp.einsum("ns,nrd->srd", match, piece_a, precision=lax.Precision.HIGHEST)
-    following_up = jnp.einsum("ns,nrf->srf", match, piece_b, precision=lax.Precision.HIGHEST)
+    count, place = (lax.axis_size("seq"), lax.axis_index("seq"))
+    left = [(i, (i - 1) % count) for i in range(count)]
+    rows = up_gradient_blocks.shape[0]
+    block = up_gradient_blocks
+    following_up = jnp.einsum(
+        "ns,nrf->srf",
+        lax.dynamic_slice_in_dim(match, place * rows, block.shape[0], axis=0),
+        block,
+        precision=lax.Precision.HIGHEST,
+    )
+    for step in range(1, count):
+        block = lax.ppermute(block, "seq", left)
+        following_up = following_up + jnp.einsum(
+            "ns,nrf->srf",
+            lax.dynamic_slice_in_dim(match, (place + step) % count * rows, block.shape[0], axis=0),
+            block,
+            precision=lax.Precision.HIGHEST,
+        )
     return (adapter_output, input_gradient, following_down, following_up)
 
 

time: 335 us -> 414 us (1.24)
  starting transfers between devices: 8.09 us -> 67.9 us
  waiting for transfers between devices: 217 us -> 236 us
  matrix products: 46.5 us -> 36.3 us
  other arithmetic: 0.67 us -> 6.09 us
  local copies, waits for them, and re-layouts: 9.04 us -> 13.3 us
    ppermute x0 -> x15, waiting for transfers between devices: none -> 79.6 us  [per_device(): block = lax.ppermute(block, 'seq', left)]
    ppermute x0 -> x15, starting transfers between devices: none -> 60.1 us  [per_device(): block = lax.ppermute(block, 'seq', left)]
    all_gather x1 -> x0, waiting for transfers between devices: 56.1 us -> none  [per_device(): piece_b = lax.all_gather(up_gradient_blocks, 'seq', axis=0, tiled=True)]
    dot_general x1 -> x0, matrix products: 9.53 us -> none  [per_device(): jnp.einsum('ns,nrf->srf', match, piece_b, precision=lax.Precision.HIGHEST)]
    add x0 -> x1, other arithmetic: none -> 5.26 us  [per_device(): following_up + jnp.einsum('ns,nrf->srf', lax.dynamic_slice_in_dim(match,...]
    all_to_all x1, waiting for transfers between devices: 6 us -> 1.03 us  [per_device(): lax.all_to_all(grad_tensor, 'tp', split_axis=0, concat_axis=1, tiled=True)]
    unnamed x11 -> x46, local copies, waits for them, and re-layouts: 5.4 us -> 9.65 us
  transfers between devices with their start and end apart: 6 -> 20, of which waited for: 4 -> 16; matrix products, arithmetic and copies ran while one was open for 6% -> 5% of each run, Pallas kernels for 0% -> 0%
where the time goes in v1:
time: 414 us; the launch traced here: 413 us
  waiting for transfers between devices  236 us (57%)
  starting transfers between devices  67.9 us (16%)
  blocking collectives  38.4 us (9%)
  matrix products  36.3 us (9%)
  between operations  15.4 us (4%)
  local copies, waits for them, and re-layouts  13.3 us (3%)
  other arithmetic  6.09 us (1%)
    all_gather x1, waiting for transfers between devices, per_device(): lax.all_gather(adapter_up, 'seq', axis=0, tiled=True)  107 us
    ppermute x15, waiting for transfers between devices, per_device(): block = lax.ppermute(block, 'seq', left)  79.6 us
    ppermute x15, starting transfers between devices, per_device(): block = lax.ppermute(block, 'seq', left)  60.1 us
    all_gather x1, waiting for transfers between devices, per_device(): lax.all_gather(adapter_down, 'seq', axis=0, tiled=True)  46.8 us
    unnamed x1, blocking collectives  30.4 us
    dot_general x1, matrix products, per_device(): jnp.einsum('ba,arf->brf', chosen_low, all_b, preferred_element_type=jnp.f...  20.9 us
    unnamed x46, local copies, waits for them, and re-layouts  9.65 us
  transfers between devices with their start and end apart: 20, of which 16 were waited for; matrix products, arithmetic and copies ran while one was open for 5% of the time, Pallas kernels for 0%

profile of v1, /device:TPU:0, one launch (start us, length us, event | category | flops | bytes accessed | tf_op | source)
XLA Modules:
  0.0 413.3 jit_solution(5628434406198278248)
XLA Ops:
  7.2 0.7 all-gather.5.cloned.1.call-update
  8.0 0.7 all-gather.7.cloned.1.call-update
  8.7 1.9 copy.58
  10.5 4.3 %all-to-all-start = ((bf16[64,2,2048]{2,0,1:T(8,128)(2,1)}), bf16[64,2,2048]{2,0,1:T(8,128)(2,1)S(1)}, u32[]{:S(2)}, u32[]{:S(2)}) async-start(bf16[64,2,2048]{2,0,1:T(8,128)(2,1)} %bitcast.95), calls=%async_computation | async-start | bytes 1048576 | tf_op jit(solution)/shard_map/all_to_all | solution.py:46
  16.4 0.1 mul.58
  16.5 46.8 %all-gather.5.cloned.1.call-done = bf16[64,16,2048]{2,1,0:T(8,128)(2,1)} async-done(((bf16[4,16,2048]{2,1,0:T(8,128)(2,1)}), bf16[64,16,2048]{2,1,0:T(8,128)(2,1)}) %all-gather.5.cloned.1.call-update) | async-done | bytes 4194320 | tf_op jit(solution)/shard_map/all_gather | solution.py:27
  63.3 6.7 %fusion.3 = bf16[1,16,2048]{2,0,1:T(2,128)(2,1)S(1)} fusion(bf16[64,16,2048]{2,1,0:T(8,128)(2,1)} %all-gather.5.cloned.1.call-done, s32[]{:T(128)} %bitcast.96), kind=kOutput, calls=%fused_computation.5 | convolution fusion | flops 4194496 | bytes 4259844 | tf_op jit(solution)/shard_map/ba,ard->brd/dot_general | solution.py:34
  70.0 0.2 convolution_bitcast_fusion.1
  70.2 0.1 copy.29
  70.3 0.1 reshape.269
  70.4 107.1 %all-gather.7.cloned.1.call-done = bf16[64,16,7168]{2,1,0:T(8,128)(2,1)} async-done(((bf16[4,16,7168]{2,1,0:T(8,128)(2,1)}), bf16[64,16,7168]{2,1,0:T(8,128)(2,1)}) %all-gather.7.cloned.1.call-update) | async-done | bytes 14680080 | tf_op jit(solution)/shard_map/all_gather | solution.py:28
  177.5 20.9 %fusion = bf16[1,16,7168]{2,0,1:T(2,128)(2,1)S(1)} fusion(bf16[64,16,7168]{2,1,0:T(8,128)(2,1)} %all-gather.7.cloned.1.call-done, s32[]{:T(128)} %bitcast.97), kind=kOutput, calls=%fused_computation | convolution fusion | flops 14680256 | bytes 14909444 | tf_op jit(solution)/shard_map/ba,arf->brf/dot_general | solution.py:37
  198.4 0.6 convolution_bitcast_fusion
  199.0 0.1 copy.30
  199.1 0.1 reshape.270
  199.2 8.1 %all-reduce.1 = (f32[1,2048]{1,0:T(1,128)S(1)}, f32[1,2048]{1,0:T(1,128)S(1)}) all-reduce(f32[1,2048]{1,0:T(1,128)S(1)} %reshape.269, f32[1,2048]{1,0:T(1,128)S(1)} %reshape.270), channel_id=1, replica_groups=mesh['seq'=16,'tp'=2] {'tp'}, use_global_device_ids=true, to_apply=%region_0.0 | all-reduce | flops 4096 | bytes 32768 | tf_op jit(solution)/shard_map/psum | solution.py:50
  207.4 0.4 convolution_multiply_fusion.1
  207.8 6.0 %collective-permute-done = f32[1,16,7168]{2,1,0:T(8,128)S(1)} collective-permute-done((f32[1,16,7168]{2,1,0:T(8,128)S(1)}, f32[1,16,7168]{2,1,0:T(8,128)S(1)}, u32[]{:S(2)}, u32[]{:S(2)}) %collective-permute-start) | collective-permute-done | bytes 458784 | tf_op jit(solution)/shard_map/ppermute | solution.py:96
  213.8 0.8 copy-done.1
  214.6 4.6 %collective-permute-start.1 = (f32[1,16,7168]{2,1,0:T(8,128)S(1)}, f32[1,16,7168]{2,1,0:T(8,128)S(1)}, u32[]{:S(2)}, u32[]{:S(2)}) collective-permute-start(f32[1,16,7168]{2,1,0:T(8,128)S(1)} %collective-permute-done), channel_id=1, source_target_pairs={{0,30},{2,0},{4,2},{6,4},{8,6},{10,8},{12,10},{14,12},{16,14},{18,... | collective-permute-start | bytes 1376264 | tf_op jit(solution)/shard_map/ppermute | solution.py:96
  219.2 6.0 %collective-permute-done.1 = f32[1,16,7168]{2,1,0:T(8,128)S(1)} collective-permute-done((f32[1,16,7168]{2,1,0:T(8,128)S(1)}, f32[1,16,7168]{2,1,0:T(8,128)S(1)}, u32[]{:S(2)}, u32[]{:S(2)}) %collective-permute-start.1) | collective-permute-done | bytes 458784 | tf_op jit(solution)/shard_map/ppermute | solution.py:96
  225.2 0.8 copy-done.3
  226.0 4.6 %collective-permute-start.2 = (f32[1,16,7168]{2,1,0:T(8,128)S(1)}, f32[1,16,7168]{2,1,0:T(8,128)S(1)}, u32[]{:S(2)}, u32[]{:S(2)}) collective-permute-start(f32[1,16,7168]{2,1,0:T(8,128)S(1)} %collective-permute-done.1), channel_id=1, source_target_pairs={{0,30},{2,0},{4,2},{6,4},{8,6},{10,8},{12,10},{14,12},{16,14},{18,... | collective-permute-start | bytes 1376264 | tf_op jit(solution)/shard_map/ppermute | solution.py:96
  230.6 6.0 %collective-permute-done.2 = f32[1,16,7168]{2,1,0:T(8,128)S(1)} collective-permute-done((f32[1,16,7168]{2,1,0:T(8,128)S(1)}, f32[1,16,7168]{2,1,0:T(8,128)S(1)}, u32[]{:S(2)}, u32[]{:S(2)}) %collective-permute-start.2) | collective-permute-done | bytes 458784 | tf_op jit(solution)/shard_map/ppermute | solution.py:96
  236.6 0.8 copy-done.5
  237.4 4.6 %collective-permute-start.3 = (f32[1,16,7168]{2,1,0:T(8,128)S(1)}, f32[1,16,7168]{2,1,0:T(8,128)S(1)}, u32[]{:S(2)}, u32[]{:S(2)}) collective-permute-start(f32[1,16,7168]{2,1,0:T(8,128)S(1)} %collective-permute-done.2), channel_id=1, source_target_pairs={{0,30},{2,0},{4,2},{6,4},{8,6},{10,8},{12,10},{14,12},{16,14},{18,... | collective-permute-start | bytes 1376264 | tf_op jit(solution)/shard_map/ppermute | solution.py:96
  242.0 6.0 %collective-permute-done.3 = f32[1,16,7168]{2,1,0:T(8,128)S(1)} collective-permute-done((f32[1,16,7168]{2,1,0:T(8,128)S(1)}, f32[1,16,7168]{2,1,0:T(8,128)S(1)}, u32[]{:S(2)}, u32[]{:S(2)}) %collective-permute-start.3) | collective-permute-done | bytes 458784 | tf_op jit(solution)/shard_map/ppermute | solution.py:96
  248.0 0.8 copy-done.7
  248.7 4.6 %collective-permute-start.4 = (f32[1,16,7168]{2,1,0:T(8,128)S(1)}, f32[1,16,7168]{2,1,0:T(8,128)}, u32[]{:S(2)}, u32[]{:S(2)}) collective-permute-start(f32[1,16,7168]{2,1,0:T(8,128)S(1)} %collective-permute-done.3), channel_id=1, source_target_pairs={{0,30},{2,0},{4,2},{6,4},{8,6},{10,8},{12,10},{14,12},{16,14},{18,... | collective-permute-start | bytes 1376264 | tf_op jit(solution)/shard_map/ppermute | solution.py:96
  253.3 6.0 %collective-permute-done.4 = f32[1,16,7168]{2,1,0:T(8,128)} collective-permute-done((f32[1,16,7168]{2,1,0:T(8,128)S(1)}, f32[1,16,7168]{2,1,0:T(8,128)}, u32[]{:S(2)}, u32[]{:S(2)}) %collective-permute-start.4) | collective-permute-done | bytes 458784 | tf_op jit(solution)/shard_map/ppermute | solution.py:96
  259.3 4.7 %collective-permute-start.5 = (f32[1,16,7168]{2,1,0:T(8,128)}, f32[1,16,7168]{2,1,0:T(8,128)}, u32[]{:S(2)}, u32[]{:S(2)}) collective-permute-start(f32[1,16,7168]{2,1,0:T(8,128)} %collective-permute-done.4), channel_id=1, source_target_pairs={{0,30},{2,0},{4,2},{6,4},{8,6},{10,8},{12,10},{14,12},{16,14},{18,... | collective-permute-start | bytes 1376264 | tf_op jit(solution)/shard_map/ppermute | solution.py:96
  264.1 6.2 %collective-permute-done.5 = f32[1,16,7168]{2,1,0:T(8,128)} collective-permute-done((f32[1,16,7168]{2,1,0:T(8,128)}, f32[1,16,7168]{2,1,0:T(8,128)}, u32[]{:S(2)}, u32[]{:S(2)}) %collective-permute-start.5) | collective-permute-done | bytes 458784 | tf_op jit(solution)/shard_map/ppermute | solution.py:96
  270.4 4.6 %collective-permute-start.6 = (f32[1,16,7168]{2,1,0:T(8,128)}, f32[1,16,7168]{2,1,0:T(8,128)}, u32[]{:S(2)}, u32[]{:S(2)}) collective-permute-start(f32[1,16,7168]{2,1,0:T(8,128)} %collective-permute-done.5), channel_id=1, source_target_pairs={{0,30},{2,0},{4,2},{6,4},{8,6},{10,8},{12,10},{14,12},{16,14},{18,... | collective-permute-start | bytes 1376264 | tf_op jit(solution)/shard_map/ppermute | solution.py:96
  275.0 0.9 fusion.47
  275.9 6.0 %collective-permute-done.6 = f32[1,16,7168]{2,1,0:T(8,128)} collective-permute-done((f32[1,16,7168]{2,1,0:T(8,128)}, f32[1,16,7168]{2,1,0:T(8,128)}, u32[]{:S(2)}, u32[]{:S(2)}) %collective-permute-start.6) | collective-permute-done | bytes 458784 | tf_op jit(solution)/shard_map/ppermute | solution.py:96
  281.9 4.6 %collective-permute-start.7 = (f32[1,16,7168]{2,1,0:T(8,128)}, f32[1,16,7168]{2,1,0:T(8,128)S(1)}, u32[]{:S(2)}, u32[]{:S(2)}) collective-permute-start(f32[1,16,7168]{2,1,0:T(8,128)} %collective-permute-done.6), channel_id=1, source_target_pairs={{0,30},{2,0},{4,2},{6,4},{8,6},{10,8},{12,10},{14,12},{16,14},{18,... | collective-permute-start | bytes 1376264 | tf_op jit(solution)/shard_map/ppermute | solution.py:96
  286.5 7.4 %collective-permute-done.7 = f32[1,16,7168]{2,1,0:T(8,128)S(1)} collective-permute-done((f32[1,16,7168]{2,1,0:T(8,128)}, f32[1,16,7168]{2,1,0:T(8,128)S(1)}, u32[]{:S(2)}, u32[]{:S(2)}) %collective-permute-start.7) | collective-permute-done | bytes 458784 | tf_op jit(solution)/shard_map/ppermute | solution.py:96
  293.9 0.8 copy-done.9
  294.7 4.5 %collective-permute-start.8 = (f32[1,16,7168]{2,1,0:T(8,128)S(1)}, f32[1,16,7168]{2,1,0:T(8,128)S(1)}, u32[]{:S(2)}, u32[]{:S(2)}) collective-permute-start(f32[1,16,7168]{2,1,0:T(8,128)S(1)} %collective-permute-done.7), channel_id=1, source_target_pairs={{0,30},{2,0},{4,2},{6,4},{8,6},{10,8},{12,10},{14,12},{16,14},{18,... | collective-permute-start | bytes 1376264 | tf_op jit(solution)/shard_map/ppermute | solution.py:96
  299.2 10.6 %collective-permute-done.8 = f32[1,16,7168]{2,1,0:T(8,128)S(1)} collective-permute-done((f32[1,16,7168]{2,1,0:T(8,128)S(1)}, f32[1,16,7168]{2,1,0:T(8,128)S(1)}, u32[]{:S(2)}, u32[]{:S(2)}) %collective-permute-start.8) | collective-permute-done | bytes 458784 | tf_op jit(solution)/shard_map/ppermute | solution.py:96
  309.8 0.8 copy-done.11
  310.6 4.7 %collective-permute-start.9 = (f32[1,16,7168]{2,1,0:T(8,128)S(1)}, f32[1,16,7168]{2,1,0:T(8,128)S(1)}, u32[]{:S(2)}, u32[]{:S(2)}) collective-permute-start(f32[1,16,7168]{2,1,0:T(8,128)S(1)} %collective-permute-done.8), channel_id=1, source_target_pairs={{0,30},{2,0},{4,2},{6,4},{8,6},{10,8},{12,10},{14,12},{16,14},{18,... | collective-permute-start | bytes 1376264 | tf_op jit(solution)/shard_map/ppermute | solution.py:96
  315.2 6.0 %collective-permute-done.9 = f32[1,16,7168]{2,1,0:T(8,128)S(1)} collective-permute-done((f32[1,16,7168]{2,1,0:T(8,128)S(1)}, f32[1,16,7168]{2,1,0:T(8,128)S(1)}, u32[]{:S(2)}, u32[]{:S(2)}) %collective-permute-start.9) | collective-permute-done | bytes 458784 | tf_op jit(solution)/shard_map/ppermute | solution.py:96
  321.2 0.8 copy-done.13
  322.0 4.6 %collective-permute-start.10 = (f32[1,16,7168]{2,1,0:T(8,128)S(1)}, f32[1,16,7168]{2,1,0:T(8,128)S(1)}, u32[]{:S(2)}, u32[]{:S(2)}) collective-permute-start(f32[1,16,7168]{2,1,0:T(8,128)S(1)} %collective-permute-done.9), channel_id=1, source_target_pairs={{0,30},{2,0},{4,2},{6,4},{8,6},{10,8},{12,10},{14,12},{16,14},{18,... | collective-permute-start | bytes 1376264 | tf_op jit(solution)/shard_map/ppermute | solution.py:96
  326.6 6.0 %collective-permute-done.10 = f32[1,16,7168]{2,1,0:T(8,128)S(1)} collective-permute-done((f32[1,16,7168]{2,1,0:T(8,128)S(1)}, f32[1,16,7168]{2,1,0:T(8,128)S(1)}, u32[]{:S(2)}, u32[]{:S(2)}) %collective-permute-start.10) | collective-permute-done | bytes 458784 | tf_op jit(solution)/shard_map/ppermute | solution.py:96
  332.6 0.8 copy-done.15
  333.4 4.6 %collective-permute-start.11 = (f32[1,16,7168]{2,1,0:T(8,128)S(1)}, f32[1,16,7168]{2,1,0:T(8,128)S(1)}, u32[]{:S(2)}, u32[]{:S(2)}) collective-permute-start(f32[1,16,7168]{2,1,0:T(8,128)S(1)} %collective-permute-done.10), channel_id=1, source_target_pairs={{0,30},{2,0},{4,2},{6,4},{8,6},{10,8},{12,10},{14,12},{16,14},{18,... | collective-permute-start | bytes 1376264 | tf_op jit(solution)/shard_map/ppermute | solution.py:96
  338.0 6.0 %collective-permute-done.11 = f32[1,16,7168]{2,1,0:T(8,128)S(1)} collective-permute-done((f32[1,16,7168]{2,1,0:T(8,128)S(1)}, f32[1,16,7168]{2,1,0:T(8,128)S(1)}, u32[]{:S(2)}, u32[]{:S(2)}) %collective-permute-start.11) | collective-permute-done | bytes 458784 | tf_op jit(solution)/shard_map/ppermute | solution.py:96
  344.0 4.6 %collective-permute-start.12 = (f32[1,16,7168]{2,1,0:T(8,128)S(1)}, f32[1,16,7168]{2,1,0:T(8,128)}, u32[]{:S(2)}, u32[]{:S(2)}) collective-permute-start(f32[1,16,7168]{2,1,0:T(8,128)S(1)} %collective-permute-done.11), channel_id=1, source_target_pairs={{0,30},{2,0},{4,2},{6,4},{8,6},{10,8},{12,10},{14,12},{16,14},{18,... | collective-permute-start | bytes 1376264 | tf_op jit(solution)/shard_map/ppermute | solution.py:96
  348.7 0.6 dynamic-slice
  349.2 0.6 fusion.26
  349.8 1.6 dynamic-update-slice
  351.5 30.4 %all-reduce = f32[16]{0:T(128)S(1)} all-reduce(f32[16]{0:T(128)S(1)} %dynamic-update-slice), channel_id=1, replica_groups=mesh['seq'=16,'tp'=2] {'seq'}, use_global_device_ids=true, to_apply=%add | all-reduce | flops 16 | bytes 128
  382.2 1.1 convolution_convert_fusion
  383.3 3.5 all-to-all-start.1
  386.8 1.4 collective-permute-done.13
  388.2 4.6 %collective-permute-start.14 = (f32[1,16,7168]{2,1,0:T(8,128)}, f32[1,16,7168]{2,1,0:T(8,128)}, u32[]{:S(2)}, u32[]{:S(2)}) collective-permute-start(f32[1,16,7168]{2,1,0:T(8,128)} %collective-permute-done.13), channel_id=1, source_target_pairs={{0,30},{2,0},{4,2},{6,4},{8,6},{10,8},{12,10},{14,12},{16,14},{18,... | collective-permute-start | bytes 1376264 | tf_op jit(solution)/shard_map/ppermute | solution.py:96
  392.8 1.8 fusion.2
  394.7 1.0 all-to-all-done.1
  395.7 0.8 copy.44
  396.6 3.7 fusion.5
  400.3 1.1 copy.34
  401.5 5.3 %multiply_add_fusion = f32[4,16,7168]{2,1,0:T(8,128)} fusion(f32[16,7168]{1,0:T(8,128)} %bitcast.48, f32[4]{0:T(128)S(1)} %get-tuple-element.37, f32[16,7168]{1,0:T(8,128)} %bitcast.46, f32[4]{0:T(128)S(1)} %get-tuple-element.23, f32[16,7168]{1,0:T(8,128)} %bitcast.44, f32[4]{0:T(128)S(1)} %get-tuple-element.24, f32[16,7168]{1,0:T(8,128)S(1)} %bitcast.116, ...), kind=kLoop, calls=%fused_computation.10 | loop fusion | flops 14221312 | bytes 9175296 | tf_op jit(solution)/shard_map/add | solution.py:97
  (56 shorter events, 0.9 us)
Async XLA Ops:
  7.2 191.2 %copy-start = (bf16[128,7168]{1,0:T(8,128)(2,1)S(1)}, bf16[128,7168]{1,0:T(8,128)(2,1)}, u32[]{:S(2)}) copy-start(bf16[128,7168]{1,0:T(8,128)(2,1)} %param.8) | copy-start | bytes 5505028
  7.2 56.1 %all-gather.5.cloned.1.call-start = ((), (), s32[]{:S(2)}) async-start(), calls=%async_computation.2 | async-start | bytes 4456448 | tf_op jit(solution)/shard_map/all_gather | solution.py:27
  7.9 169.6 %all-gather.7.cloned.1.call-start = ((), (), s32[]{:S(2)}) async-start(), calls=%async_computation.3 | async-start | bytes 15597568 | tf_op jit(solution)/shard_map/all_gather | solution.py:28
  10.5 59.4 %all-to-all-start = ((bf16[64,2,2048]{2,0,1:T(8,128)(2,1)}), bf16[64,2,2048]{2,0,1:T(8,128)(2,1)S(1)}, u32[]{:S(2)}, u32[]{:S(2)}) async-start(bf16[64,2,2048]{2,0,1:T(8,128)(2,1)} %bitcast.95), calls=%async_computation | async-start | bytes 1048576 | tf_op jit(solution)/shard_map/all_to_all | solution.py:46
  14.8 381.7 %all-gather.9.cloned.1.call-start = ((), (), s32[]{:S(2)}) async-start(), calls=%async_computation.4 | async-start | bytes 2228224 | tf_op jit(solution)/shard_map/all_gather | solution.py:81
  199.0 149.7 %copy-start.20 = (u32[32]{0:T(128)S(1)}, u32[32]{0:T(128)}, u32[]{:S(2)}) copy-start(u32[32]{0:T(128)} %constant.117) | copy-start | bytes 388
  199.0 150.3 %copy-start.19 = (s32[64]{0:T(128)S(1)}, s32[64]{0:T(128)}, u32[]{:S(2)}) copy-start(s32[64]{0:T(128)} %param.13) | copy-start | bytes 772
  207.8 6.0 %collective-permute-start = (f32[1,16,7168]{2,1,0:T(8,128)S(1)}, f32[1,16,7168]{2,1,0:T(8,128)S(1)}, u32[]{:S(2)}, u32[]{:S(2)}) collective-permute-start(f32[1,16,7168]{2,1,0:T(8,128)S(1)} %bitcast.105), channel_id=1, source_target_pairs={{0,30},{2,0},{4,2},{6,4},{8,6},{10,8},{12,10},{14,12},{16,14},{18,... | collective-permute-start | bytes 1376264 | tf_op jit(solution)/shard_map/ppermute | solution.py:96
  213.8 0.8 copy-start.1
  214.6 10.6 %collective-permute-start.1 = (f32[1,16,7168]{2,1,0:T(8,128)S(1)}, f32[1,16,7168]{2,1,0:T(8,128)S(1)}, u32[]{:S(2)}, u32[]{:S(2)}) collective-permute-start(f32[1,16,7168]{2,1,0:T(8,128)S(1)} %collective-permute-done), channel_id=1, source_target_pairs={{0,30},{2,0},{4,2},{6,4},{8,6},{10,8},{12,10},{14,12},{16,14},{18,... | collective-permute-start | bytes 1376264 | tf_op jit(solution)/shard_map/ppermute | solution.py:96
  225.2 0.8 copy-start.3
  226.0 10.6 %collective-permute-start.2 = (f32[1,16,7168]{2,1,0:T(8,128)S(1)}, f32[1,16,7168]{2,1,0:T(8,128)S(1)}, u32[]{:S(2)}, u32[]{:S(2)}) collective-permute-start(f32[1,16,7168]{2,1,0:T(8,128)S(1)} %collective-permute-done.1), channel_id=1, source_target_pairs={{0,30},{2,0},{4,2},{6,4},{8,6},{10,8},{12,10},{14,12},{16,14},{18,... | collective-permute-start | bytes 1376264 | tf_op jit(solution)/shard_map/ppermute | solution.py:96
  236.6 0.8 copy-start.5
  237.4 10.6 %collective-permute-start.3 = (f32[1,16,7168]{2,1,0:T(8,128)S(1)}, f32[1,16,7168]{2,1,0:T(8,128)S(1)}, u32[]{:S(2)}, u32[]{:S(2)}) collective-permute-start(f32[1,16,7168]{2,1,0:T(8,128)S(1)} %collective-permute-done.2), channel_id=1, source_target_pairs={{0,30},{2,0},{4,2},{6,4},{8,6},{10,8},{12,10},{14,12},{16,14},{18,... | collective-permute-start | bytes 1376264 | tf_op jit(solution)/shard_map/ppermute | solution.py:96
  248.0 0.8 copy-start.7
  248.7 10.6 %collective-permute-start.4 = (f32[1,16,7168]{2,1,0:T(8,128)S(1)}, f32[1,16,7168]{2,1,0:T(8,128)}, u32[]{:S(2)}, u32[]{:S(2)}) collective-permute-start(f32[1,16,7168]{2,1,0:T(8,128)S(1)} %collective-permute-done.3), channel_id=1, source_target_pairs={{0,30},{2,0},{4,2},{6,4},{8,6},{10,8},{12,10},{14,12},{16,14},{18,... | collective-permute-start | bytes 1376264 | tf_op jit(solution)/shard_map/ppermute | solution.py:96
  259.3 11.0 %collective-permute-start.5 = (f32[1,16,7168]{2,1,0:T(8,128)}, f32[1,16,7168]{2,1,0:T(8,128)}, u32[]{:S(2)}, u32[]{:S(2)}) collective-permute-start(f32[1,16,7168]{2,1,0:T(8,128)} %collective-permute-done.4), channel_id=1, source_target_pairs={{0,30},{2,0},{4,2},{6,4},{8,6},{10,8},{12,10},{14,12},{16,14},{18,... | collective-permute-start | bytes 1376264 | tf_op jit(solution)/shard_map/ppermute | solution.py:96
  270.4 11.5 %collective-permute-start.6 = (f32[1,16,7168]{2,1,0:T(8,128)}, f32[1,16,7168]{2,1,0:T(8,128)}, u32[]{:S(2)}, u32[]{:S(2)}) collective-permute-start(f32[1,16,7168]{2,1,0:T(8,128)} %collective-permute-done.5), channel_id=1, source_target_pairs={{0,30},{2,0},{4,2},{6,4},{8,6},{10,8},{12,10},{14,12},{16,14},{18,... | collective-permute-start | bytes 1376264 | tf_op jit(solution)/shard_map/ppermute | solution.py:96
  281.9 12.0 %collective-permute-start.7 = (f32[1,16,7168]{2,1,0:T(8,128)}, f32[1,16,7168]{2,1,0:T(8,128)S(1)}, u32[]{:S(2)}, u32[]{:S(2)}) collective-permute-start(f32[1,16,7168]{2,1,0:T(8,128)} %collective-permute-done.6), channel_id=1, source_target_pairs={{0,30},{2,0},{4,2},{6,4},{8,6},{10,8},{12,10},{14,12},{16,14},{18,... | collective-permute-start | bytes 1376264 | tf_op jit(solution)/shard_map/ppermute | solution.py:96
  293.9 0.8 copy-start.9
  294.7 15.1 %collective-permute-start.8 = (f32[1,16,7168]{2,1,0:T(8,128)S(1)}, f32[1,16,7168]{2,1,0:T(8,128)S(1)}, u32[]{:S(2)}, u32[]{:S(2)}) collective-permute-start(f32[1,16,7168]{2,1,0:T(8,128)S(1)} %collective-permute-done.7), channel_id=1, source_target_pairs={{0,30},{2,0},{4,2},{6,4},{8,6},{10,8},{12,10},{14,12},{16,14},{18,... | collective-permute-start | bytes 1376264 | tf_op jit(solution)/shard_map/ppermute | solution.py:96
  309.8 0.8 copy-start.11
  310.6 10.7 %collective-permute-start.9 = (f32[1,16,7168]{2,1,0:T(8,128)S(1)}, f32[1,16,7168]{2,1,0:T(8,128)S(1)}, u32[]{:S(2)}, u32[]{:S(2)}) collective-permute-start(f32[1,16,7168]{2,1,0:T(8,128)S(1)} %collective-permute-done.8), channel_id=1, source_target_pairs={{0,30},{2,0},{4,2},{6,4},{8,6},{10,8},{12,10},{14,12},{16,14},{18,... | collective-permute-start | bytes 1376264 | tf_op jit(solution)/shard_map/ppermute | solution.py:96
  321.2 0.8 copy-start.13
  322.0 10.6 %collective-permute-start.10 = (f32[1,16,7168]{2,1,0:T(8,128)S(1)}, f32[1,16,7168]{2,1,0:T(8,128)S(1)}, u32[]{:S(2)}, u32[]{:S(2)}) collective-permute-start(f32[1,16,7168]{2,1,0:T(8,128)S(1)} %collective-permute-done.9), channel_id=1, source_target_pairs={{0,30},{2,0},{4,2},{6,4},{8,6},{10,8},{12,10},{14,12},{16,14},{18,... | collective-permute-start | bytes 1376264 | tf_op jit(solution)/shard_map/ppermute | solution.py:96
  332.6 0.8 copy-start.15
  333.4 10.6 %collective-permute-start.11 = (f32[1,16,7168]{2,1,0:T(8,128)S(1)}, f32[1,16,7168]{2,1,0:T(8,128)S(1)}, u32[]{:S(2)}, u32[]{:S(2)}) collective-permute-start(f32[1,16,7168]{2,1,0:T(8,128)S(1)} %collective-permute-done.10), channel_id=1, source_target_pairs={{0,30},{2,0},{4,2},{6,4},{8,6},{10,8},{12,10},{14,12},{16,14},{18,... | collective-permute-start | bytes 1376264 | tf_op jit(solution)/shard_map/ppermute | solution.py:96
  344.0 39.3 %copy-start.17 = (f32[1,16,7168]{2,1,0:T(8,128)}, f32[1,16,7168]{2,1,0:T(8,128)S(1)}, u32[]{:S(2)}) copy-start(f32[1,16,7168]{2,1,0:T(8,128)S(1)} %collective-permute-done.11) | copy-start | bytes 1376260
  344.0 37.9 %collective-permute-start.12 = (f32[1,16,7168]{2,1,0:T(8,128)S(1)}, f32[1,16,7168]{2,1,0:T(8,128)}, u32[]{:S(2)}, u32[]{:S(2)}) collective-permute-start(f32[1,16,7168]{2,1,0:T(8,128)S(1)} %collective-permute-done.11), channel_id=1, source_target_pairs={{0,30},{2,0},{4,2},{6,4},{8,6},{10,8},{12,10},{14,12},{16,14},{18,... | collective-permute-start | bytes 1376264 | tf_op jit(solution)/shard_map/ppermute | solution.py:96
  381.9 6.4 %collective-permute-start.13 = (f32[1,16,7168]{2,1,0:T(8,128)}, f32[1,16,7168]{2,1,0:T(8,128)}, u32[]{:S(2)}, u32[]{:S(2)}) collective-permute-start(f32[1,16,7168]{2,1,0:T(8,128)} %collective-permute-done.12), channel_id=1, source_target_pairs={{0,30},{2,0},{4,2},{6,4},{8,6},{10,8},{12,10},{14,12},{16,14},{18,... | collective-permute-start | bytes 1376264 | tf_op jit(solution)/shard_map/ppermute | solution.py:96
  383.3 12.4 %all-to-all-start.1 = ((bf16[2,64,2048]{2,1,0:T(8,128)(2,1)}), bf16[2,64,2048]{2,1,0:T(8,128)(2,1)S(1)}, u32[]{:S(2)}, u32[]{:S(2)}) async-start(bf16[2,64,2048]{2,1,0:T(8,128)(2,1)} %bitcast.10), calls=%async_computation.1 | async-start | bytes 1048576 | tf_op jit(solution)/shard_map/all_to_all | solution.py:63
  388.2 13.2 %collective-permute-start.14 = (f32[1,16,7168]{2,1,0:T(8,128)}, f32[1,16,7168]{2,1,0:T(8,128)}, u32[]{:S(2)}, u32[]{:S(2)}) collective-permute-start(f32[1,16,7168]{2,1,0:T(8,128)} %collective-permute-done.13), channel_id=1, source_target_pairs={{0,30},{2,0},{4,2},{6,4},{8,6},{10,8},{12,10},{14,12},{16,14},{18,... | collective-permute-start | bytes 1376264 | tf_op jit(solution)/shard_map/ppermute | solution.py:96
  395.7 5.7 %copy-start.18 = (f32[1,16,7168]{2,1,0:T(8,128)S(1)}, f32[1,16,7168]{2,1,0:T(8,128)}, u32[]{:S(2)}) copy-start(f32[1,16,7168]{2,1,0:T(8,128)} %copy-done.17) | copy-start | bytes 1376260
  396.6 4.9 %copy-start.2 = (f32[1,16,7168]{2,1,0:T(8,128)S(1)}, f32[1,16,7168]{2,1,0:T(8,128)}, u32[]{:S(2)}) copy-start(f32[1,16,7168]{2,1,0:T(8,128)} %copy-done.1) | copy-start | bytes 1376260
  396.6 4.9 %copy-start.4 = (f32[1,16,7168]{2,1,0:T(8,128)S(1)}, f32[1,16,7168]{2,1,0:T(8,128)}, u32[]{:S(2)}) copy-start(f32[1,16,7168]{2,1,0:T(8,128)} %copy-done.3) | copy-start | bytes 1376260
  396.6 4.9 %copy-start.6 = (f32[1,16,7168]{2,1,0:T(8,128)S(1)}, f32[1,16,7168]{2,1,0:T(8,128)}, u32[]{:S(2)}) copy-start(f32[1,16,7168]{2,1,0:T(8,128)} %copy-done.5) | copy-start | bytes 1376260
  396.6 4.9 %copy-start.8 = (f32[1,16,7168]{2,1,0:T(8,128)S(1)}, f32[1,16,7168]{2,1,0:T(8,128)}, u32[]{:S(2)}) copy-start(f32[1,16,7168]{2,1,0:T(8,128)} %copy-done.7) | copy-start | bytes 1376260
  396.6 4.9 %copy-start.10 = (f32[1,16,7168]{2,1,0:T(8,128)S(1)}, f32[1,16,7168]{2,1,0:T(8,128)}, u32[]{:S(2)}) copy-start(f32[1,16,7168]{2,1,0:T(8,128)} %copy-done.9) | copy-start | bytes 1376260
  396.6 4.9 %copy-start.12 = (f32[1,16,7168]{2,1,0:T(8,128)S(1)}, f32[1,16,7168]{2,1,0:T(8,128)}, u32[]{:S(2)}) copy-start(f32[1,16,7168]{2,1,0:T(8,128)} %copy-done.11) | copy-start | bytes 1376260
  396.6 4.9 %copy-start.14 = (f32[1,16,7168]{2,1,0:T(8,128)S(1)}, f32[1,16,7168]{2,1,0:T(8,128)}, u32[]{:S(2)}) copy-start(f32[1,16,7168]{2,1,0:T(8,128)} %copy-done.13) | copy-start | bytes 1376260
  396.6 4.9 %copy-start.16 = (f32[1,16,7168]{2,1,0:T(8,128)S(1)}, f32[1,16,7168]{2,1,0:T(8,128)}, u32[]{:S(2)}) copy-start(f32[1,16,7168]{2,1,0:T(8,128)} %copy-done.15) | copy-start | bytes 1376260
Sparse Core Ops, SparseCore 0:
  10.1 53.0 all-gather.4
  65.6 111.8 all-gather.6
  276.0 42.7 all-gather.8
